TPU v7x, 128 devices: a whole 4x4x4 slice. The times are simulated.
128 devices in a mesh: width: 4 (over z), row: 4 (over y), src: 8 (over x, core).
Axes of the slice: x: 4, y: 4, z: 4, core: 2. Of those that a mesh axis runs over, the one named last changes fastest.
Arguments:
- query_rows: bfloat16 [1024, 8192], P('row', 'width'), may hold values from -150 to 150
- key_rows: bfloat16 [1024, 1024], P('src', 'width'), may hold values from -7 to 7
- value_rows: bfloat16 [1024, 1024], P('src'), may hold values from -6 to 6
- out_proj: bfloat16 [8192, 8192], P(('row', 'src'), 'width'), may hold values from -0.0625 to 0.0625
Outputs:
- share: float32 [1024, 1024], P('row', ('src', 'width'))
All inputs are finite; a program needn't handle non-finite values.
Results may differ from a plain program's by a relative error of at most 0.0014.
Values may be sent and summed in bfloat16 or wider, within the bound.
A program may use at most 192 MiB of HBM per device.

v0:
```python
import math
import jax
import jax.numpy as jnp
from jax import lax
from jax.sharding import PartitionSpec as P

H = 64
KV = 8
HD = 128


def sent_to_all(shard, axis):
    copies = jnp.broadcast_to(shard, (lax.axis_size(axis), *shard.shape))
    return lax.all_to_all(copies, axis, split_axis=0, concat_axis=0, tiled=True)


def gathered_once(shard, axis):
    leaves = jax.tree.leaves(shard)
    sequence = sorted(range(len(leaves)), key=lambda k: -leaves[k].size)
    width = (1, *leaves[sequence[0]].shape)[-1]
    lines = [
        jnp.pad(leaves[k].reshape(-1), (0, -leaves[k].size % width)).reshape(-1, width)
        for k in sequence
    ]
    both, at, found = (sent_to_all(jnp.concatenate(lines), axis), 0, {})
    for k, line in zip(sequence, lines):
        slab = both[:, at : at + len(line)].reshape(len(both), -1)
        found[k] = slab[:, : leaves[k].size].reshape(-1, *leaves[k].shape)
        at += len(line)
    numbers = iter(range(len(leaves)))
    return jax.tree.map(lambda _: found[next(numbers)], shard)


def combined_pairwise(pieces, combine):
    while len(jax.tree.leaves(pieces)[0]) > 1:
        pieces = jax.vmap(combine)(
            *(jax.tree.map(lambda part: part[side::2], pieces) for side in (0, 1))
        )
    return jax.tree.map(lambda part: part[0], pieces)


def merged(shard, axis, combine):
    pieces = gathered_once(shard, axis)
    return combined_pairwise(pieces, combine)


def cut_along(shard, dim, size):
    dims = shard.shape
    parts = shard.reshape(*dims[:dim], size, dims[dim] // size, *dims[dim + 1 :])
    return jnp.moveaxis(parts, dim, 0)


def sum_at_owner(shard, axis, dim):
    size = lax.axis_size(axis)
    parts = lax.all_to_all(cut_along(shard, dim, size), axis, 0, 0, tiled=True)
    return jnp.sum(parts, axis=0)


def of_everyone(shard, axis):
    return sent_to_all(shard, axis).sum(axis=0)


def combine_stats(first, second):
    peak_one, mass_one = first
    peak_two, mass_two = second
    larger = jnp.maximum(peak_one, peak_two)
    return (larger, mass_one * jnp.exp(peak_one - larger) + mass_two * jnp.exp(peak_two - larger))


def body(query_rows, key_rows, value_rows, out_proj):
    here_row = lax.axis_index("row")
    here_src = lax.axis_index("src")
    row_count = query_rows.shape[0]
    col_count = key_rows.shape[0]
    group_size = H // KV
    row_pos = here_row * row_count + jnp.arange(row_count, dtype=jnp.int32)
    col_pos = here_src * col_count + jnp.arange(col_count, dtype=jnp.int32)
    local_heads = query_rows.shape[1] // HD
    local_kv = key_rows.shape[1] // HD
    queries = query_rows.reshape(row_count, local_kv, group_size, HD)
    key_heads = key_rows.reshape(col_count, local_kv, HD)
    scores = jnp.einsum("ikgd,jkd->kgij", queries, key_heads, preferred_element_type=jnp.float32)
    scores = scores.reshape(local_heads, row_count, col_count) / jnp.sqrt(jnp.float32(HD))
    causal = row_pos[:, None] >= col_pos[None, :]
    masked = jnp.where(causal, scores, jnp.float32(-1e30))
    row_peak = jnp.max(masked, axis=-1)
    row_mass = jnp.sum(jnp.where(causal, jnp.exp(masked - row_peak[..., None]), 0.0), axis=-1)
    row_peak, row_mass = merged((row_peak, row_mass), "src", combine_stats)
    weights = jnp.where(
        causal, jnp.exp(masked - row_peak[..., None]) / row_mass[..., None], 0.0
    ).astype(jnp.bfloat16)
    weights = lax.all_gather(weights, "width", axis=0, tiled=True)
    value_heads = value_rows.reshape(col_count, KV, HD)
    out_cols = out_proj.shape[1]
    proj_heads = out_proj.reshape(-1, HD, out_cols)
    portion = lax.all_gather(proj_heads, ("row", "src"), axis=0, tiled=True)
    head_count = portion.shape[0]
    head_ids = jnp.arange(head_count, dtype=jnp.int32)
    selector = (head_ids[:, None] // group_size == jnp.arange(KV, dtype=jnp.int32)[None, :]).astype(
        jnp.bfloat16
    )
    chosen = jnp.einsum(
        "hk,jkd->jhd", selector, value_heads, preferred_element_type=jnp.float32
    ).astype(jnp.bfloat16)
    images = jnp.einsum("jhd,hde->jhe", chosen, portion, preferred_element_type=jnp.float32).astype(
        jnp.bfloat16
    )
    row_block = math.gcd(row_count, 64)
    col_block = math.gcd(col_count, 32)
    col_steps = col_count // col_block
    turns = row_count // row_block * col_steps

    def tile(turn_index, running):
        row_start = turn_index // col_steps * row_block
        col_start = turn_index % col_steps * col_block
        row_slice = lax.dynamic_slice_in_dim(row_pos, row_start, row_block)
        col_slice = lax.dynamic_slice_in_dim(col_pos, col_start, col_block)

        def compute(unused):
            attend = lax.dynamic_slice(
                weights, (0, row_start, col_start), (H, row_block, col_block)
            )
            source_images = lax.dynamic_slice_in_dim(images, col_start, col_block, 0)
            contrib = jnp.einsum(
                "hij,jhe->ije", attend, source_images, preferred_element_type=jnp.float32
            )
            return jnp.sum(jnp.abs(contrib), axis=-1)

        def skipped(unused):
            return jnp.zeros((row_block, col_block), jnp.float32)

        result = lax.cond(jnp.max(row_slice) >= jnp.min(col_slice), compute, skipped, 0)
        return lax.dynamic_update_slice(running, result, (row_start, col_start))

    partial_value = lax.fori_loop(0, turns, tile, jnp.zeros((row_count, col_count), jnp.float32))
    summed = sum_at_owner(partial_value, "width", 1)
    totals = of_everyone(jnp.sum(summed, axis=1), ("width", "src"))
    position = (here_row * row_count + jnp.arange(row_count, dtype=jnp.int32) + 1).astype(
        jnp.float32
    )
    return position[:, None] * summed / totals[:, None]


def solution(mesh):
    placed = (P("row", "width"), P("src", "width"), P("src", None), P(("row", "src"), "width"))
    return jax.shard_map(
        body, mesh=mesh, in_specs=placed, out_specs=P("row", ("src", "width")), check_vma=False
    )
```

profile of v0, /device:TPU:25, one launch (start us, length us, event | category | flops | bytes accessed | tf_op | source)
XLA Modules:
  0.0 431.4 jit_solution(18067964968503341397)
XLA Ops:
  27.2 47.7 %all-gather.5.cloned.1.call-done = bf16[64,256,128]{2,1,0:T(8,128)(2,1)} async-done(((bf16[16,256,128]{2,1,0:T(8,128)(2,1)}), bf16[64,256,128]{2,1,0:T(8,128)(2,1)}) %all-gather.5.cloned.1.call-update) | async-done | bytes 4194320 | tf_op jit(solution)/shard_map/all_gather | solution.py:92
  75.0 15.6 %copy.29 = bf16[64,256,128]{0,1,2:T(8,128)(2,1)} copy(bf16[64,256,128]{2,1,0:T(8,128)(2,1)} %all-gather.5.cloned.1.call-done) | data formatting | bytes 8388608 | tf_op jit(solution)/shard_map/while | solution.py:135
  90.6 100.2 %all-gather.3.cloned.1.call-done = bf16[64,128,2048]{2,1,0:T(8,128)(2,1)} async-done(((bf16[2,128,2048]{2,1,0:T(8,128)(2,1)}), bf16[64,128,2048]{2,1,0:T(8,128)(2,1)}) %all-gather.3.cloned.1.call-update) | async-done | bytes 33554448 | tf_op jit(solution)/shard_map/all_gather | solution.py:96
  190.8 24.2 %convert_bitcast_fusion = bf16[128,64,2048]{2,0,1:T(8,128)(2,1)} fusion(bf16[64,128,2048]{2,1,0:T(8,128)(2,1)} %all-gather.3.cloned.1.call-done, bf16[128,64,128]{2,1,0:T(8,128)(2,1)S(1)} %convert_bitcast_fusion.1), kind=kOutput, calls=%fused_computation.7 | convolution fusion | flops 4311744512 | bytes 69206016 | tf_op jit(solution)/shard_map/jhd,hde->jhe/dot_general | solution.py:105
  215.0 30.0 %copy.28 = bf16[128,64,2048]{2,1,0:T(8,128)(2,1)} copy(bf16[128,64,2048]{2,0,1:T(8,128)(2,1)} %convert_bitcast_fusion) | data formatting | bytes 67108864 | tf_op jit(solution)/shard_map/while | solution.py:135
  245.0 156.7 %while.15 = (s32[]{:T(128)}, f32[256,128]{0,1:T(8,128)S(1)}, s32[256]{0:T(256)S(1)}, s32[128]{0:T(128)S(1)}, bf16[128,64,2048]{2,1,0:T(8,128)(2,1)}, /*index=5*/...) while((s32[]{:T(128)}, f32[256,128]{0,1:T(8,128)S(1)}, ...), condition=%wide.region_8.9_spmd, body=%wide.region_2.8_spmd.sunk | while | flops 545257600 | bytes 8939898 | solution.py:135
  247.9 6.0 %conditional.2 = (f32[64,32]{0,1:T(8,128)S(1)}) conditional(s32[]{:T(128)} %convert_element_type.44, () %tuple.54, (s32[]{:T(128)}, bf16[128,64,2048]{2,1,0:T(8,128)(2,1)}, s32[]{:T(128)}, bf16[64,256,128]{0,1,2:T(8,128)(2,1)}) %tuple.55), branch_computations={%region_5.5_spmd, %region_6.7_spmd} | conditional | flops 545257472 | bytes 8922700 | solution.py:132
  257.7 6.0 %conditional.2 = (f32[64,32]{0,1:T(8,128)S(1)}) conditional(s32[]{:T(128)} %convert_element_type.44, () %tuple.54, (s32[]{:T(128)}, bf16[128,64,2048]{2,1,0:T(8,128)(2,1)}, s32[]{:T(128)}, bf16[64,256,128]{0,1,2:T(8,128)(2,1)}) %tuple.55), branch_computations={%region_5.5_spmd, %region_6.7_spmd} | conditional | flops 545257472 | bytes 8922700 | solution.py:132
  267.5 6.0 %conditional.2 = (f32[64,32]{0,1:T(8,128)S(1)}) conditional(s32[]{:T(128)} %convert_element_type.44, () %tuple.54, (s32[]{:T(128)}, bf16[128,64,2048]{2,1,0:T(8,128)(2,1)}, s32[]{:T(128)}, bf16[64,256,128]{0,1,2:T(8,128)(2,1)}) %tuple.55), branch_computations={%region_5.5_spmd, %region_6.7_spmd} | conditional | flops 545257472 | bytes 8922700 | solution.py:132
  277.3 6.0 %conditional.2 = (f32[64,32]{0,1:T(8,128)S(1)}) conditional(s32[]{:T(128)} %convert_element_type.44, () %tuple.54, (s32[]{:T(128)}, bf16[128,64,2048]{2,1,0:T(8,128)(2,1)}, s32[]{:T(128)}, bf16[64,256,128]{0,1,2:T(8,128)(2,1)}) %tuple.55), branch_computations={%region_5.5_spmd, %region_6.7_spmd} | conditional | flops 545257472 | bytes 8922700 | solution.py:132
  286.9 6.0 %conditional.2 = (f32[64,32]{0,1:T(8,128)S(1)}) conditional(s32[]{:T(128)} %convert_element_type.44, () %tuple.54, (s32[]{:T(128)}, bf16[128,64,2048]{2,1,0:T(8,128)(2,1)}, s32[]{:T(128)}, bf16[64,256,128]{0,1,2:T(8,128)(2,1)}) %tuple.55), branch_computations={%region_5.5_spmd, %region_6.7_spmd} | conditional | flops 545257472 | bytes 8922700 | solution.py:132
  297.0 6.0 %conditional.2 = (f32[64,32]{0,1:T(8,128)S(1)}) conditional(s32[]{:T(128)} %convert_element_type.44, () %tuple.54, (s32[]{:T(128)}, bf16[128,64,2048]{2,1,0:T(8,128)(2,1)}, s32[]{:T(128)}, bf16[64,256,128]{0,1,2:T(8,128)(2,1)}) %tuple.55), branch_computations={%region_5.5_spmd, %region_6.7_spmd} | conditional | flops 545257472 | bytes 8922700 | solution.py:132
  307.0 6.0 %conditional.2 = (f32[64,32]{0,1:T(8,128)S(1)}) conditional(s32[]{:T(128)} %convert_element_type.44, () %tuple.54, (s32[]{:T(128)}, bf16[128,64,2048]{2,1,0:T(8,128)(2,1)}, s32[]{:T(128)}, bf16[64,256,128]{0,1,2:T(8,128)(2,1)}) %tuple.55), branch_computations={%region_5.5_spmd, %region_6.7_spmd} | conditional | flops 545257472 | bytes 8922700 | solution.py:132
  317.1 6.0 %conditional.2 = (f32[64,32]{0,1:T(8,128)S(1)}) conditional(s32[]{:T(128)} %convert_element_type.44, () %tuple.54, (s32[]{:T(128)}, bf16[128,64,2048]{2,1,0:T(8,128)(2,1)}, s32[]{:T(128)}, bf16[64,256,128]{0,1,2:T(8,128)(2,1)}) %tuple.55), branch_computations={%region_5.5_spmd, %region_6.7_spmd} | conditional | flops 545257472 | bytes 8922700 | solution.py:132
  327.0 6.0 %conditional.2 = (f32[64,32]{0,1:T(8,128)S(1)}) conditional(s32[]{:T(128)} %convert_element_type.44, () %tuple.54, (s32[]{:T(128)}, bf16[128,64,2048]{2,1,0:T(8,128)(2,1)}, s32[]{:T(128)}, bf16[64,256,128]{0,1,2:T(8,128)(2,1)}) %tuple.55), branch_computations={%region_5.5_spmd, %region_6.7_spmd} | conditional | flops 545257472 | bytes 8922700 | solution.py:132
  336.6 6.0 %conditional.2 = (f32[64,32]{0,1:T(8,128)S(1)}) conditional(s32[]{:T(128)} %convert_element_type.44, () %tuple.54, (s32[]{:T(128)}, bf16[128,64,2048]{2,1,0:T(8,128)(2,1)}, s32[]{:T(128)}, bf16[64,256,128]{0,1,2:T(8,128)(2,1)}) %tuple.55), branch_computations={%region_5.5_spmd, %region_6.7_spmd} | conditional | flops 545257472 | bytes 8922700 | solution.py:132
  346.2 6.0 %conditional.2 = (f32[64,32]{0,1:T(8,128)S(1)}) conditional(s32[]{:T(128)} %convert_element_type.44, () %tuple.54, (s32[]{:T(128)}, bf16[128,64,2048]{2,1,0:T(8,128)(2,1)}, s32[]{:T(128)}, bf16[64,256,128]{0,1,2:T(8,128)(2,1)}) %tuple.55), branch_computations={%region_5.5_spmd, %region_6.7_spmd} | conditional | flops 545257472 | bytes 8922700 | solution.py:132
  355.8 6.0 %conditional.2 = (f32[64,32]{0,1:T(8,128)S(1)}) conditional(s32[]{:T(128)} %convert_element_type.44, () %tuple.54, (s32[]{:T(128)}, bf16[128,64,2048]{2,1,0:T(8,128)(2,1)}, s32[]{:T(128)}, bf16[64,256,128]{0,1,2:T(8,128)(2,1)}) %tuple.55), branch_computations={%region_5.5_spmd, %region_6.7_spmd} | conditional | flops 545257472 | bytes 8922700 | solution.py:132
  365.2 6.0 %conditional.2 = (f32[64,32]{0,1:T(8,128)S(1)}) conditional(s32[]{:T(128)} %convert_element_type.44, () %tuple.54, (s32[]{:T(128)}, bf16[128,64,2048]{2,1,0:T(8,128)(2,1)}, s32[]{:T(128)}, bf16[64,256,128]{0,1,2:T(8,128)(2,1)}) %tuple.55), branch_computations={%region_5.5_spmd, %region_6.7_spmd} | conditional | flops 545257472 | bytes 8922700 | solution.py:132
  375.1 6.0 %conditional.2 = (f32[64,32]{0,1:T(8,128)S(1)}) conditional(s32[]{:T(128)} %convert_element_type.44, () %tuple.54, (s32[]{:T(128)}, bf16[128,64,2048]{2,1,0:T(8,128)(2,1)}, s32[]{:T(128)}, bf16[64,256,128]{0,1,2:T(8,128)(2,1)}) %tuple.55), branch_computations={%region_5.5_spmd, %region_6.7_spmd} | conditional | flops 545257472 | bytes 8922700 | solution.py:132
  384.9 6.0 %conditional.2 = (f32[64,32]{0,1:T(8,128)S(1)}) conditional(s32[]{:T(128)} %convert_element_type.44, () %tuple.54, (s32[]{:T(128)}, bf16[128,64,2048]{2,1,0:T(8,128)(2,1)}, s32[]{:T(128)}, bf16[64,256,128]{0,1,2:T(8,128)(2,1)}) %tuple.55), branch_computations={%region_5.5_spmd, %region_6.7_spmd} | conditional | flops 545257472 | bytes 8922700 | solution.py:132
  394.8 6.0 %conditional.2 = (f32[64,32]{0,1:T(8,128)S(1)}) conditional(s32[]{:T(128)} %convert_element_type.44, () %tuple.54, (s32[]{:T(128)}, bf16[128,64,2048]{2,1,0:T(8,128)(2,1)}, s32[]{:T(128)}, bf16[64,256,128]{0,1,2:T(8,128)(2,1)}) %tuple.55), branch_computations={%region_5.5_spmd, %region_6.7_spmd} | conditional | flops 545257472 | bytes 8922700 | solution.py:132
  401.7 8.7 %all_to_all.16 = f32[4,256,32]{1,2,0:T(8,128)S(1)} all-to-all(f32[4,256,32]{1,2,0:T(8,128)S(1)} %bitcast.40), channel_id=1, replica_groups=mesh['width'=4,'row'=4,'src'=8] {'width'}, dimensions={0} | all-to-all | bytes 262144 | tf_op jit(solution)/shard_map/all_to_all | solution.py:55
  416.6 7.2 %all-to-all-done.2 = f32[32,1,256]{2,1,0:T(1,128)S(1)} async-done(((f32[32,1,256]{2,1,0:T(1,128)}), f32[32,1,256]{2,1,0:T(1,128)S(1)}, u32[]{:S(2)}, u32[]{:S(2)}) %all-to-all-start.2) | async-done | bytes 32800 | tf_op jit(solution)/shard_map/all_to_all | solution.py:14
  (100 shorter events, 161.9 us)
Async XLA Ops:
  6.5 1.5 copy-start.1
  10.0 11.5 %all-to-all-start = ((f32[8,32,256]{2,1,0:T(8,128)}), f32[8,32,256]{2,1,0:T(8,128)S(1)}, u32[]{:S(2)}, u32[]{:S(2)}) async-start(f32[8,32,256]{2,1,0:T(8,128)} %broadcast_in_dim.44), calls=%async_computation | async-start | bytes 524288 | tf_op jit(solution)/shard_map/all_to_all | solution.py:14
  14.9 60.0 %all-gather.5.cloned.1.call-start = ((), (), s32[]{:S(2)}) async-start(), calls=%async_computation.4 | async-start | bytes 5242880 | tf_op jit(solution)/shard_map/all_gather | solution.py:92
  21.6 4.9 %copy-start = (bf16[128,1024]{1,0:T(8,128)(2,1)S(1)}, bf16[128,1024]{1,0:T(8,128)(2,1)}, u32[]{:S(2)}) copy-start(bf16[128,1024]{1,0:T(8,128)(2,1)} %param.10) | copy-start | bytes 786436
  25.7 165.1 %all-gather.3.cloned.1.call-start = ((), (), s32[]{:S(2)}) async-start(), calls=%async_computation.3 | async-start | bytes 34603008 | tf_op jit(solution)/shard_map/all_gather | solution.py:96
  411.1 12.8 %all-to-all-start.2 = ((f32[32,1,256]{2,1,0:T(1,128)}), f32[32,1,256]{2,1,0:T(1,128)S(1)}, u32[]{:S(2)}, u32[]{:S(2)}) async-start(f32[32,1,256]{2,1,0:T(1,128)} %broadcast_in_dim.46), calls=%async_computation.2 | async-start | bytes 65536 | tf_op jit(solution)/shard_map/all_to_all | solution.py:14
Sparse Core Ops, SparseCore 0:
  25.8 49.1 all-gather.4
  77.2 113.4 all-gather.2
where the time goes:
time: 432 us; the launch traced here: 431 us
  waiting for transfers between devices  160 us (37%)
  matrix products  122 us (28%)
  local copies, waits for them, and re-layouts  64.2 us (15%)
  other arithmetic  30.2 us (7%)
  loops' own time  22.2 us (5%)
  between operations  13.6 us (3%)
  starting transfers between devices  10.8 us (2%)
  blocking collectives  8.75 us (2%)
    all_gather x1, waiting for transfers between devices, body(): portion = lax.all_gather(proj_heads, ('row', 'src'), axis=0, tiled=True)  100 us
    dot_general x16, matrix products, compute(): jnp.einsum('hij,jhe->ije', attend, source_images, preferred_element_type=...  96.1 us
    all_gather x1, waiting for transfers between devices, body(): weights = lax.all_gather(weights, 'width', axis=0, tiled=True)  47.7 us
    while x2, local copies, waits for them, and re-layouts, body(): lax.fori_loop(0, turns, tile, jnp.zeros((row_count, col_count), jnp.float...  45.6 us
    dot_general x1, matrix products, body(): jnp.einsum('jhd,hde->jhe', chosen, portion, preferred_element_type=jnp.fl...  24.2 us
    another operation x1, loops' own time, body(): lax.fori_loop(0, turns, tile, jnp.zeros((row_count, col_count), jnp.float...  21.8 us
    dynamic_update_slice x16, local copies, waits for them, and re-layouts, tile(): return lax.dynamic_update_slice(running, result, (row_start, col_start))  13.7 us
    reduce_max x16, other arithmetic, tile(): jnp.max(row_slice) >= jnp.min(col_slice)  12.5 us
  transfers between devices with their start and end apart: 4, of which 4 were waited for; matrix products, arithmetic and copies ran while one was open for 4% of the time, Pallas kernels for 0%

commit v1 on v0

--- a/solution.py
+++ b/solution.py
@@ -89,7 +89,14 @@
     weights = jnp.where(
         causal, jnp.exp(masked - row_peak[..., None]) / row_mass[..., None], 0.0
     ).astype(jnp.bfloat16)
-    weights = lax.all_gather(weights, "width", axis=0, tiled=True)
+    ring = [weights]
+    for hop in range(3):
+        ring.append(lax.ppermute(ring[-1], "width", [(dev, (dev + 1) % 4) for dev in range(4)]))
+    weights = jnp.roll(
+        jnp.concatenate(ring[::-1], axis=0),
+        (lax.axis_index("width") + 1) * ring[0].shape[0],
+        axis=0,
+    )
     value_heads = value_rows.reshape(col_count, KV, HD)
     out_cols = out_proj.shape[1]
     proj_heads = out_proj.reshape(-1, HD, out_cols)

time: 432 us -> 369 us (0.85)
  waiting for transfers between devices: 160 us -> 81.8 us
  local copies, waits for them, and re-layouts: 64.2 us -> 73.8 us
    all_gather x1, waiting for transfers between devices: 100 us -> 0.01 us  [body(): portion = lax.all_gather(proj_heads, ('row', 'src'), axis=0, tiled=True)]
    ppermute x0 -> x3, waiting for transfers between devices: none -> 69.4 us  [body(): lax.ppermute(ring[-1], 'width', [(dev, (dev + 1) % 4) for dev in range(4)])]
    all_gather x1 -> x0, waiting for transfers between devices: 47.7 us -> none  [body(): weights = lax.all_gather(weights, 'width', axis=0, tiled=True)]
    unnamed x6 -> x14, local copies, waits for them, and re-layouts: 1.53 us -> 8.37 us
  transfers between devices with their start and end apart: 4 -> 6, of which waited for: 4 -> 5; matrix products, arithmetic and copies ran while one was open for 4% -> 10% of each run, Pallas kernels for 0% -> 0%
where the time goes in v1:
time: 369 us; the launch traced here: 368 us
  matrix products  123 us (33%)
  waiting for transfers between devices  81.8 us (22%)
  local copies, waits for them, and re-layouts  73.8 us (20%)
  other arithmetic  30.7 us (8%)
  loops' own time  22.2 us (6%)
  starting transfers between devices  14.1 us (4%)
  between operations  13.7 us (4%)
  blocking collectives  8.38 us (2%)
    dot_general x16, matrix products, compute(): jnp.einsum('hij,jhe->ije', attend, source_images, preferred_element_type=...  96.1 us
    ppermute x3, waiting for transfers between devices, body(): lax.ppermute(ring[-1], 'width', [(dev, (dev + 1) % 4) for dev in range(4)])  69.4 us
    while x2, local copies, waits for them, and re-layouts, body(): lax.fori_loop(0, turns, tile, jnp.zeros((row_count, col_count), jnp.float...  45.9 us
    dot_general x1, matrix products, body(): jnp.einsum('jhd,hde->jhe', chosen, portion, preferred_element_type=jnp.fl...  24.2 us
    another operation x1, loops' own time, body(): lax.fori_loop(0, turns, tile, jnp.zeros((row_count, col_count), jnp.float...  21.8 us
    dynamic_update_slice x16, local copies, waits for them, and re-layouts, tile(): return lax.dynamic_update_slice(running, result, (row_start, col_start))  13.7 us
    reduce_max x16, other arithmetic, tile(): jnp.max(row_slice) >= jnp.min(col_slice)  12.5 us
    all_to_all x2, starting transfers between devices, sent_to_all(): return lax.all_to_all(copies, axis, split_axis=0, concat_axis=0, tiled=True)  12.4 us
  transfers between devices with their start and end apart: 6, of which 5 were waited for; matrix products, arithmetic and copies ran while one was open for 10% of the time, Pallas kernels for 0%

profile of v1, /device:TPU:25, one launch (start us, length us, event | category | flops | bytes accessed | tf_op | source)
XLA Modules:
  0.0 367.6 jit_solution(17169989095466100934)
XLA Ops:
  25.4 24.6 %collective-permute-done = bf16[16,256,128]{2,1,0:T(8,128)(2,1)S(1)} collective-permute-done((bf16[16,256,128]{2,1,0:T(8,128)(2,1)S(1)}, bf16[16,256,128]{2,1,0:T(8,128)(2,1)S(1)}, u32[]{:S(2)}, u32[]{:S(2)}) %collective-permute-start) | collective-permute-done | bytes 1048608 | tf_op jit(solution)/shard_map/ppermute | solution.py:94
  50.0 24.3 %collective-permute-done.1 = bf16[16,256,128]{2,1,0:T(8,128)(2,1)} collective-permute-done((bf16[16,256,128]{2,1,0:T(8,128)(2,1)S(1)}, bf16[16,256,128]{2,1,0:T(8,128)(2,1)}, u32[]{:S(2)}, u32[]{:S(2)}) %collective-permute-start.1) | collective-permute-done | bytes 1048608 | tf_op jit(solution)/shard_map/ppermute | solution.py:94
  77.4 20.5 %collective-permute-done.2 = bf16[16,256,128]{2,1,0:T(8,128)(2,1)} collective-permute-done((bf16[16,256,128]{2,1,0:T(8,128)(2,1)}, bf16[16,256,128]{2,1,0:T(8,128)(2,1)}, u32[]{:S(2)}, u32[]{:S(2)}) %collective-permute-start.2) | collective-permute-done | bytes 1048608 | tf_op jit(solution)/shard_map/ppermute | solution.py:94
  109.6 15.9 %copy.29 = bf16[64,256,128]{0,1,2:T(8,128)(2,1)} copy(bf16[64,256,128]{2,1,0:T(8,128)(2,1)} %constant_dynamic-slice_fusion) | data formatting | bytes 8388608 | tf_op jit(solution)/shard_map/while | solution.py:142
  125.5 24.2 %convert_bitcast_fusion = bf16[128,64,2048]{2,0,1:T(8,128)(2,1)} fusion(bf16[64,128,2048]{2,1,0:T(8,128)(2,1)} %all-gather.2.cloned.1.call-done, bf16[128,64,128]{2,1,0:T(8,128)(2,1)S(1)} %copy-done.1), kind=kOutput, calls=%fused_computation.7 | convolution fusion | flops 4311744512 | bytes 69206016 | tf_op jit(solution)/shard_map/jhd,hde->jhe/dot_general | solution.py:112
  149.7 30.0 %copy.28 = bf16[128,64,2048]{2,1,0:T(8,128)(2,1)} copy(bf16[128,64,2048]{2,0,1:T(8,128)(2,1)} %convert_bitcast_fusion) | data formatting | bytes 67108864 | tf_op jit(solution)/shard_map/while | solution.py:142
  179.7 156.7 %while.15 = (s32[]{:T(128)}, f32[256,128]{0,1:T(8,128)S(1)}, s32[256]{0:T(256)S(1)}, s32[128]{0:T(128)S(1)}, bf16[128,64,2048]{2,1,0:T(8,128)(2,1)}, /*index=5*/...) while((s32[]{:T(128)}, f32[256,128]{0,1:T(8,128)S(1)}, ...), condition=%wide.region_8.9_spmd, body=%wide.region_2.8_spmd.sunk | while | flops 545257600 | bytes 8939898 | solution.py:142
  182.6 6.0 %conditional.2 = (f32[64,32]{0,1:T(8,128)S(1)}) conditional(s32[]{:T(128)} %convert_element_type.48, () %tuple.54, (s32[]{:T(128)}, bf16[128,64,2048]{2,1,0:T(8,128)(2,1)}, s32[]{:T(128)}, bf16[64,256,128]{0,1,2:T(8,128)(2,1)}) %tuple.55), branch_computations={%region_5.5_spmd, %region_6.7_spmd} | conditional | flops 545257472 | bytes 8922700 | solution.py:139
  192.4 6.0 %conditional.2 = (f32[64,32]{0,1:T(8,128)S(1)}) conditional(s32[]{:T(128)} %convert_element_type.48, () %tuple.54, (s32[]{:T(128)}, bf16[128,64,2048]{2,1,0:T(8,128)(2,1)}, s32[]{:T(128)}, bf16[64,256,128]{0,1,2:T(8,128)(2,1)}) %tuple.55), branch_computations={%region_5.5_spmd, %region_6.7_spmd} | conditional | flops 545257472 | bytes 8922700 | solution.py:139
  202.2 6.0 %conditional.2 = (f32[64,32]{0,1:T(8,128)S(1)}) conditional(s32[]{:T(128)} %convert_element_type.48, () %tuple.54, (s32[]{:T(128)}, bf16[128,64,2048]{2,1,0:T(8,128)(2,1)}, s32[]{:T(128)}, bf16[64,256,128]{0,1,2:T(8,128)(2,1)}) %tuple.55), branch_computations={%region_5.5_spmd, %region_6.7_spmd} | conditional | flops 545257472 | bytes 8922700 | solution.py:139
  212.0 6.0 %conditional.2 = (f32[64,32]{0,1:T(8,128)S(1)}) conditional(s32[]{:T(128)} %convert_element_type.48, () %tuple.54, (s32[]{:T(128)}, bf16[128,64,2048]{2,1,0:T(8,128)(2,1)}, s32[]{:T(128)}, bf16[64,256,128]{0,1,2:T(8,128)(2,1)}) %tuple.55), branch_computations={%region_5.5_spmd, %region_6.7_spmd} | conditional | flops 545257472 | bytes 8922700 | solution.py:139
  221.6 6.0 %conditional.2 = (f32[64,32]{0,1:T(8,128)S(1)}) conditional(s32[]{:T(128)} %convert_element_type.48, () %tuple.54, (s32[]{:T(128)}, bf16[128,64,2048]{2,1,0:T(8,128)(2,1)}, s32[]{:T(128)}, bf16[64,256,128]{0,1,2:T(8,128)(2,1)}) %tuple.55), branch_computations={%region_5.5_spmd, %region_6.7_spmd} | conditional | flops 545257472 | bytes 8922700 | solution.py:139
  231.6 6.0 %conditional.2 = (f32[64,32]{0,1:T(8,128)S(1)}) conditional(s32[]{:T(128)} %convert_element_type.48, () %tuple.54, (s32[]{:T(128)}, bf16[128,64,2048]{2,1,0:T(8,128)(2,1)}, s32[]{:T(128)}, bf16[64,256,128]{0,1,2:T(8,128)(2,1)}) %tuple.55), branch_computations={%region_5.5_spmd, %region_6.7_spmd} | conditional | flops 545257472 | bytes 8922700 | solution.py:139
  241.7 6.0 %conditional.2 = (f32[64,32]{0,1:T(8,128)S(1)}) conditional(s32[]{:T(128)} %convert_element_type.48, () %tuple.54, (s32[]{:T(128)}, bf16[128,64,2048]{2,1,0:T(8,128)(2,1)}, s32[]{:T(128)}, bf16[64,256,128]{0,1,2:T(8,128)(2,1)}) %tuple.55), branch_computations={%region_5.5_spmd, %region_6.7_spmd} | conditional | flops 545257472 | bytes 8922700 | solution.py:139
  251.8 6.0 %conditional.2 = (f32[64,32]{0,1:T(8,128)S(1)}) conditional(s32[]{:T(128)} %convert_element_type.48, () %tuple.54, (s32[]{:T(128)}, bf16[128,64,2048]{2,1,0:T(8,128)(2,1)}, s32[]{:T(128)}, bf16[64,256,128]{0,1,2:T(8,128)(2,1)}) %tuple.55), branch_computations={%region_5.5_spmd, %region_6.7_spmd} | conditional | flops 545257472 | bytes 8922700 | solution.py:139
  261.7 6.0 %conditional.2 = (f32[64,32]{0,1:T(8,128)S(1)}) conditional(s32[]{:T(128)} %convert_element_type.48, () %tuple.54, (s32[]{:T(128)}, bf16[128,64,2048]{2,1,0:T(8,128)(2,1)}, s32[]{:T(128)}, bf16[64,256,128]{0,1,2:T(8,128)(2,1)}) %tuple.55), branch_computations={%region_5.5_spmd, %region_6.7_spmd} | conditional | flops 545257472 | bytes 8922700 | solution.py:139
  271.3 6.0 %conditional.2 = (f32[64,32]{0,1:T(8,128)S(1)}) conditional(s32[]{:T(128)} %convert_element_type.48, () %tuple.54, (s32[]{:T(128)}, bf16[128,64,2048]{2,1,0:T(8,128)(2,1)}, s32[]{:T(128)}, bf16[64,256,128]{0,1,2:T(8,128)(2,1)}) %tuple.55), branch_computations={%region_5.5_spmd, %region_6.7_spmd} | conditional | flops 545257472 | bytes 8922700 | solution.py:139
  280.9 6.0 %conditional.2 = (f32[64,32]{0,1:T(8,128)S(1)}) conditional(s32[]{:T(128)} %convert_element_type.48, () %tuple.54, (s32[]{:T(128)}, bf16[128,64,2048]{2,1,0:T(8,128)(2,1)}, s32[]{:T(128)}, bf16[64,256,128]{0,1,2:T(8,128)(2,1)}) %tuple.55), branch_computations={%region_5.5_spmd, %region_6.7_spmd} | conditional | flops 545257472 | bytes 8922700 | solution.py:139
  290.4 6.0 %conditional.2 = (f32[64,32]{0,1:T(8,128)S(1)}) conditional(s32[]{:T(128)} %convert_element_type.48, () %tuple.54, (s32[]{:T(128)}, bf16[128,64,2048]{2,1,0:T(8,128)(2,1)}, s32[]{:T(128)}, bf16[64,256,128]{0,1,2:T(8,128)(2,1)}) %tuple.55), branch_computations={%region_5.5_spmd, %region_6.7_spmd} | conditional | flops 545257472 | bytes 8922700 | solution.py:139
  319.6 6.0 %conditional.2 = (f32[64,32]{0,1:T(8,128)S(1)}) conditional(s32[]{:T(128)} %convert_element_type.48, () %tuple.54, (s32[]{:T(128)}, bf16[128,64,2048]{2,1,0:T(8,128)(2,1)}, s32[]{:T(128)}, bf16[64,256,128]{0,1,2:T(8,128)(2,1)}) %tuple.55), branch_computations={%region_5.5_spmd, %region_6.7_spmd} | conditional | flops 545257472 | bytes 8922700 | solution.py:139
  329.5 6.0 %conditional.2 = (f32[64,32]{0,1:T(8,128)S(1)}) conditional(s32[]{:T(128)} %convert_element_type.48, () %tuple.54, (s32[]{:T(128)}, bf16[128,64,2048]{2,1,0:T(8,128)(2,1)}, s32[]{:T(128)}, bf16[64,256,128]{0,1,2:T(8,128)(2,1)}) %tuple.55), branch_computations={%region_5.5_spmd, %region_6.7_spmd} | conditional | flops 545257472 | bytes 8922700 | solution.py:139
  336.3 8.4 %all_to_all.16 = f32[4,256,32]{1,2,0:T(8,128)S(1)} all-to-all(f32[4,256,32]{1,2,0:T(8,128)S(1)} %bitcast.40), channel_id=1, replica_groups=mesh['width'=4,'row'=4,'src'=8] {'width'}, dimensions={0} | all-to-all | bytes 262144 | tf_op jit(solution)/shard_map/all_to_all | solution.py:55
  345.4 7.4 %all-to-all-start.2 = ((f32[32,1,256]{2,1,0:T(1,128)}), f32[32,1,256]{2,1,0:T(1,128)S(1)}, u32[]{:S(2)}, u32[]{:S(2)}) async-start(f32[32,1,256]{2,1,0:T(1,128)} %broadcast_in_dim.46), calls=%async_computation.2 | async-start | bytes 65536 | tf_op jit(solution)/shard_map/all_to_all | solution.py:14
  352.8 7.2 %all-to-all-done.2 = f32[32,1,256]{2,1,0:T(1,128)S(1)} async-done(((f32[32,1,256]{2,1,0:T(1,128)}), f32[32,1,256]{2,1,0:T(1,128)S(1)}, u32[]{:S(2)}, u32[]{:S(2)}) %all-to-all-start.2) | async-done | bytes 32800 | tf_op jit(solution)/shard_map/all_to_all | solution.py:14
  (114 shorter events, 181.3 us)
Async XLA Ops:
  6.5 2.2 copy-start.2
  6.5 119.0 %all-gather.2.cloned.1.call-start = ((), (), s32[]{:S(2)}) async-start(), calls=%async_computation.3 | async-start | bytes 34603008 | tf_op jit(solution)/shard_map/all_gather | solution.py:103
  9.5 6.5 %copy-start = (f32[2,128,256,8]{2,1,3,0:T(8,128)}, f32[2,128,256,8]{2,1,3,0:T(8,128)S(1)}, u32[]{:S(2)}) copy-start(f32[2,128,256,8]{2,1,3,0:T(8,128)S(1)} %get-tuple-element.232) | copy-start | bytes 6291460
  10.9 11.5 %all-to-all-start = ((f32[8,32,256]{2,1,0:T(8,128)}), f32[8,32,256]{2,1,0:T(8,128)S(1)}, u32[]{:S(2)}, u32[]{:S(2)}) async-start(f32[8,32,256]{2,1,0:T(8,128)} %broadcast_in_dim.44), calls=%async_computation | async-start | bytes 524288 | tf_op jit(solution)/shard_map/all_to_all | solution.py:14
  23.7 26.3 %collective-permute-start = (bf16[16,256,128]{2,1,0:T(8,128)(2,1)S(1)}, bf16[16,256,128]{2,1,0:T(8,128)(2,1)S(1)}, u32[]{:S(2)}, u32[]{:S(2)}) collective-permute-start(bf16[16,256,128]{2,1,0:T(8,128)(2,1)S(1)} %select_convert_fusion), channel_id=1, source_target_pairs={{0,32},{32,64},{64,96},{96,0},{1,33},{33,65},{65,97},{97,1},{2,34}... | collective-permute-start | bytes 3145736 | tf_op jit(solution)/shard_map/ppermute | solution.py:94
  50.0 24.3 %collective-permute-start.1 = (bf16[16,256,128]{2,1,0:T(8,128)(2,1)S(1)}, bf16[16,256,128]{2,1,0:T(8,128)(2,1)}, u32[]{:S(2)}, u32[]{:S(2)}) collective-permute-start(bf16[16,256,128]{2,1,0:T(8,128)(2,1)S(1)} %collective-permute-done), channel_id=1, source_target_pairs={{0,32},{32,64},{64,96},{96,0},{1,33},{33,65},{65,97},{97,1},{2,34}... | collective-permute-start | bytes 3145736 | tf_op jit(solution)/shard_map/ppermute | solution.py:94
  74.4 23.6 %collective-permute-start.2 = (bf16[16,256,128]{2,1,0:T(8,128)(2,1)}, bf16[16,256,128]{2,1,0:T(8,128)(2,1)}, u32[]{:S(2)}, u32[]{:S(2)}) collective-permute-start(bf16[16,256,128]{2,1,0:T(8,128)(2,1)} %collective-permute-done.1), channel_id=1, source_target_pairs={{0,32},{32,64},{64,96},{96,0},{1,33},{33,65},{65,97},{97,1},{2,34}... | collective-permute-start | bytes 3145736 | tf_op jit(solution)/shard_map/ppermute | solution.py:94
  109.6 15.9 %copy-start.1 = (bf16[128,64,128]{2,1,0:T(8,128)(2,1)S(1)}, bf16[128,64,128]{2,1,0:T(8,128)(2,1)}, u32[]{:S(2)}) copy-start(bf16[128,64,128]{2,1,0:T(8,128)(2,1)} %convert_bitcast_fusion.1) | copy-start | bytes 6291460
  345.4 14.6 %all-to-all-start.2 = ((f32[32,1,256]{2,1,0:T(1,128)}), f32[32,1,256]{2,1,0:T(1,128)S(1)}, u32[]{:S(2)}, u32[]{:S(2)}) async-start(f32[32,1,256]{2,1,0:T(1,128)} %broadcast_in_dim.46), calls=%async_computation.2 | async-start | bytes 65536 | tf_op jit(solution)/shard_map/all_to_all | solution.py:14
Sparse Core Ops, SparseCore 0:
  9.6 115.4 all-gather.1
